TPU v7x, 128 devices: a whole 4x4x4 slice. The times are simulated.
128 devices in a mesh: outer: 8 (over y, core), inner: 16 (over z, x).
Axes of the slice: x: 4, y: 4, z: 4, core: 2. Of those that a mesh axis runs over, the one named last changes fastest.
Arguments:
- queries: bfloat16 [16384, 2048], P(('outer', 'inner')), may hold values from -6 to 6
- key_vectors: bfloat16 [16384, 2048], P(('outer', 'inner')), may hold values from -6 to 6
- value_vectors: bfloat16 [16384, 2048], P(('outer', 'inner')), may hold values from -6 to 6
- segment_ids: int32 [16384], P(('outer', 'inner')), may hold values from 0 to 15, never falling along the last dimension, each value on 1 to 4096 neighbouring positions
- ridge_weight: float32 [16], replicated, may hold values from 2 to 32
Outputs:
- readout: float32 [16384, 2048], P(('outer', 'inner'))
Inputs may be any that keep to these rules, and one draw needn't show every extreme that they name: `segment_ids`: segment ids never fall along the sequence; each document has 1 to 4096 tokens and one has exactly 4096.
All inputs are finite; a program needn't handle non-finite values.
Results may differ from a plain program's by a relative error of at most 0.0003.
Values sent between devices are 32-bit elements; how exact they have to be, the bound alone decides.
A program may use at most 128 MiB of HBM per device.

v0:
```python
import jax
import jax.numpy as jnp
from jax import lax
from jax.sharding import PartitionSpec as P

CG_ITERS = 3


highest = lax.Precision.HIGHEST


def prefix_2(value, axis, join, neutral):
    count, mine = (lax.axis_size(axis), lax.axis_index(axis))
    pieces = jax.tree.map(lambda part: lax.all_gather(part, axis), value)
    running = jax.tree.map(
        lambda part, zero: jnp.full_like(part, 0) + jnp.asarray(zero, part.dtype), value, neutral
    )

    def hop(position, running):
        longer = join(running, jax.tree.map(lambda part: part[position], pieces))
        return jax.tree.map(lambda new, old: jnp.where(position < mine, new, old), longer, running)

    return lax.fori_loop(0, count - 1, hop, running)


def from_root(shard, axis, root):
    mine = lax.axis_index(axis) == root
    return lax.psum(jnp.where(mine, shard, jnp.zeros_like(shard)), axis)


def normed(values_in):
    widened = values_in.astype(jnp.float32)
    return widened * lax.rsqrt(jnp.sum(widened * widened, -1, keepdims=True) + 1e-06)


def combine(earlier, latter):
    early_last, early_gram, early_cross = earlier
    late_last, late_gram, late_cross = latter
    keep_mask = jnp.logical_or(early_last == late_last, late_last < 0).astype(jnp.float32)
    return (
        jnp.where(late_last < 0, early_last, late_last),
        late_gram + keep_mask * early_gram,
        late_cross + keep_mask * early_cross,
    )


def summarize(key_rows, value_rows, segment):
    last_value = segment[-1]
    weight = (segment == last_value).astype(jnp.float32)[None, :, None]
    gram = jnp.einsum("hbe,hbf->hef", key_rows * weight, key_rows, precision=highest)
    cross = jnp.einsum("hbv,hbk->hvk", value_rows * weight, key_rows, precision=highest)
    return (last_value.astype(jnp.float32), gram, cross)


def span_solve(query_rows, key_rows, value_rows, segment, prefix, ridge_weight):
    prev_last, gram_in, cross_in = prefix
    segment_value = segment.astype(jnp.float32)
    carried = (segment_value == prev_last).astype(jnp.float32)[None, :, None]
    position = jnp.arange(segment.shape[0])
    within = jnp.logical_and(
        position[:, None] >= position[None, :], segment[:, None] == segment[None, :]
    ).astype(jnp.float32)[None]
    solved = jnp.zeros_like(query_rows)
    remain = query_rows
    search = query_rows
    remain_square = jnp.sum(remain * remain, -1, keepdims=True)
    for _ in range(CG_ITERS):
        apply_from_state = jnp.einsum("hbf,hef->hbe", search, gram_in, precision=highest) * carried
        apply_scores = jnp.einsum("hte,hse->hts", search, key_rows, precision=highest) * within
        local_part = jnp.einsum("hts,hse->hte", apply_scores, key_rows, precision=highest)
        applied = apply_from_state + local_part + ridge_weight[:, None, None] * search
        stepsize = remain_square / jnp.sum(search * applied, -1, keepdims=True)
        solved = solved + stepsize * search
        remain = remain - stepsize * applied
        next_square = jnp.sum(remain * remain, -1, keepdims=True)
        search = remain + next_square / remain_square * search
        remain_square = next_square
    from_state = jnp.einsum("hbk,hvk->hbv", solved, cross_in, precision=highest) * carried
    scores = jnp.einsum("hte,hse->hts", solved, key_rows, precision=highest) * within
    return from_state + jnp.einsum("hts,hsv->htv", scores, value_rows, precision=highest)


def on_device(queries, key_vectors, value_vectors, segment_ids, ridge_weight):
    row_count = queries.shape[0]
    head_count = ridge_weight.shape[0]
    head_width = queries.shape[1] // head_count

    def split_heads(values_in):
        return values_in.reshape(row_count, head_count, head_width).transpose(1, 0, 2)

    query_rows = normed(split_heads(queries))
    key_rows = normed(split_heads(key_vectors))
    value_rows = split_heads(value_vectors).astype(jnp.float32)
    own = summarize(key_rows, value_rows, segment_ids)
    zeros_state = jnp.zeros((head_count, head_width, head_width), jnp.float32)
    identity = (jnp.float32(-1.0), zeros_state, zeros_state)
    within_group = prefix_2(own, "inner", combine, identity)
    inclusive = combine(within_group, own)
    totals = (
        from_root(inclusive[0], "inner", lax.axis_size("inner") - 1),
        from_root(inclusive[1], "inner", lax.axis_size("inner") - 1),
        from_root(inclusive[2], "inner", lax.axis_size("inner") - 1),
    )
    before = prefix_2(totals, "outer", combine, identity)
    prefix = combine(before, within_group)
    result = span_solve(query_rows, key_rows, value_rows, segment_ids, prefix, ridge_weight)
    return result.transpose(1, 0, 2).reshape(row_count, head_count * head_width)


def solution(mesh):
    in_specs = (
        P(("outer", "inner"), None),
        P(("outer", "inner"), None),
        P(("outer", "inner"), None),
        P(("outer", "inner")),
        P(),
    )
    out_specs = P(("outer", "inner"), None)
    return jax.shard_map(
        on_device, mesh=mesh, in_specs=in_specs, out_specs=out_specs, check_vma=False
    )
```

profile of v0, /device:TPU:0, one launch (start us, length us, event | category | flops | bytes accessed | tf_op | source)
XLA Modules:
  0.0 597.3 jit_solution(4818602046917445556)
XLA Ops:
  11.9 3.2 fusion.13
  15.2 3.2 fusion.4
  21.3 42.6 %all-reduce = f32[16]{0:T(128)S(1)} all-reduce(f32[16]{0:T(128)S(1)} %dynamic-update-slice), channel_id=1, replica_groups=mesh['outer'=8,'inner'=16] {'inner'}, use_global_device_ids=true, to_apply=%add | all-reduce | flops 16 | bytes 128
  63.9 65.4 %all-gather.13.cloned.1.call-done = f32[256,128,128]{2,1,0:T(8,128)} async-done(((f32[16,128,128]{2,1,0:T(8,128)}), f32[256,128,128]{2,1,0:T(8,128)}) %all-gather.13.cloned.1.call-update) | async-done | bytes 16777232 | tf_op jit(solution)/shard_map/all_gather | solution.py:14
  129.3 113.0 %all-gather.11.cloned.1.call-done = f32[256,128,128]{2,1,0:T(8,128)} async-done(((f32[16,128,128]{2,1,0:T(8,128)}), f32[256,128,128]{2,1,0:T(8,128)}) %all-gather.11.cloned.1.call-update) | async-done | bytes 16777232 | tf_op jit(solution)/shard_map/all_gather | solution.py:14
  242.3 80.3 %while.36 = (s32[]{:T(128)}, f32[]{:T(128)}, f32[16,128,128]{2,1,0:T(8,128)S(1)}, f32[16,128,128]{2,1,0:T(8,128)S(1)}, s32[]{:T(128)}, /*index=5*/f32[16]{0:T(12...) while((s32[]{:T(128)}, f32[]{:T(128)}, ...), condition=%wide.region_4.5_spmd.clone, body=%wide.region_3.4_spmd.clone.sunk | while | flops 2097162 | bytes 6291657 | solution.py:23
  255.1 2.6 fusion.59
  287.1 2.7 fusion.59
  308.6 2.7 fusion.59
  322.7 3.6 select_bitcast_fusion
  326.4 91.1 %all-reduce.5.cloned.1.call-done = (f32[1,16,128,128]{3,2,1,0:T(8,128)}, f32[1,16,128,128]{3,2,1,0:T(8,128)}) async-done(((f32[1,16,128,128]{3,2,1,0:T(8,128)}, f32[1,16,128,128]{3,2,1,0:T(8,128)}), (f32[1,16,128,128]{3,2,1,0:T(8,128)}, f32[1,16,128,128]{3,2,1,0:T(8,128)})) %all-reduce.5.cloned.1.call-update) | async-done | bytes 2097168 | tf_op jit(solution)/shard_map/psum | solution.py:28
  420.3 2.9 convolution_multiply_fusion.6
  423.1 39.4 %psum.21 = f32[1]{0:T(128)} all-reduce(f32[1]{0:T(128)} %bitcast.13), channel_id=1, replica_groups=mesh['outer'=8,'inner'=16] {'inner'}, use_global_device_ids=true, to_apply=%region_5.6 | all-reduce | flops 1 | bytes 8 | tf_op jit(solution)/shard_map/psum | solution.py:28
  463.9 12.4 %all-reduce.1 = f32[8]{0:T(128)S(1)} all-reduce(f32[8]{0:T(128)S(1)} %dynamic-update-slice.1), channel_id=1, replica_groups=mesh['outer'=8,'inner'=16] {'outer'}, use_global_device_ids=true, to_apply=%add.1 | all-reduce | flops 8 | bytes 64
  476.3 43.4 %all-gather.9.cloned.1.call-done = f32[8,16,128,128]{3,2,1,0:T(8,128)} async-done(((f32[1,16,128,128]{3,2,1,0:T(8,128)}), f32[8,16,128,128]{3,2,1,0:T(8,128)}) %all-gather.9.cloned.1.call-update) | async-done | bytes 8388624 | tf_op jit(solution)/shard_map/all_gather | solution.py:14
  519.7 46.0 %while.37 = (s32[]{:T(128)}, f32[]{:T(128)}, f32[16,128,128]{2,1,0:T(8,128)}, f32[16,128,128]{2,1,0:T(8,128)}, s32[]{:T(128)}, /*index=5*/f32[8]{0:T(128)S(1)}, ...) while((s32[]{:T(128)}, f32[]{:T(128)}, ...), condition=%wide.region_9.10_spmd.clone, body=%wide.region_8.9_spmd.clone.sunk | while | flops 2097162 | bytes 6291657 | solution.py:23
  521.7 3.4 fusion.60
  527.7 4.1 fusion.60
  534.3 4.1 fusion.60
  540.9 4.1 fusion.60
  547.6 4.1 fusion.60
  554.2 4.1 fusion.60
  560.8 4.1 fusion.60
  568.6 3.7 multiply_reduce_fusion.3
  (102 shorter events, 78.5 us)
Async XLA Ops:
  6.5 122.8 %all-gather.13.cloned.1.call-start = ((), (), s32[]{:S(2)}) async-start(), calls=%async_computation.3 | async-start | bytes 17825792 | tf_op jit(solution)/shard_map/all_gather | solution.py:14
  11.8 52.0 %copy-start.2 = (bf16[128,2048]{0,1:T(8,128)(2,1)}, bf16[128,2048]{0,1:T(8,128)(2,1)S(1)}, u32[]{:S(2)}) copy-start(bf16[128,2048]{0,1:T(8,128)(2,1)S(1)} %copy.33) | copy-start | bytes 1572868
  15.1 227.2 %all-gather.11.cloned.1.call-start = ((), (), s32[]{:S(2)}) async-start(), calls=%async_computation.2 | async-start | bytes 17825792 | tf_op jit(solution)/shard_map/all_gather | solution.py:14
  18.4 399.1 %all-reduce.5.cloned.1.call-start = ((), (), s32[]{:S(2)}) async-start(), calls=%async_computation.4 | async-start | bytes 4194304 | tf_op jit(solution)/shard_map/psum | solution.py:28
  242.3 175.8 %copy-start.6 = (u32[128]{0:T(128)S(1)}, u32[128]{0:T(128)}, u32[]{:S(2)}) copy-start(u32[128]{0:T(128)} %constant.83) | copy-start | bytes 1540
  242.3 177.8 %copy-start.5 = (s32[128]{0:T(128)S(1)}, s32[128]{0:T(128)}, u32[]{:S(2)}) copy-start(s32[128]{0:T(128)} %param.12) | copy-start | bytes 1540
  322.7 96.1 %copy-start = (f32[16,128,128]{2,1,0:T(8,128)}, f32[16,128,128]{2,1,0:T(8,128)S(1)}, u32[]{:S(2)}) copy-start(f32[16,128,128]{2,1,0:T(8,128)S(1)} %get-tuple-element.287) | copy-start | bytes 3145732
  326.3 150.0 %all-gather.7.cloned.1.call-start = ((), (), s32[]{:S(2)}) async-start(), calls=%async_computation | async-start | bytes 9437184 | tf_op jit(solution)/shard_map/all_gather | solution.py:14
  417.5 102.2 %all-gather.9.cloned.1.call-start = ((), (), s32[]{:S(2)}) async-start(), calls=%async_computation.1 | async-start | bytes 9437184 | tf_op jit(solution)/shard_map/all_gather | solution.py:14
  519.7 48.9 %copy-start.4 = (f32[16]{0:T(128)S(1)}, f32[16]{0:T(128)}, u32[]{:S(2)}) copy-start(f32[16]{0:T(128)} %param.13) | copy-start | bytes 196
  574.7 12.4 %copy-start.1 = (f32[16,128,128]{2,1,0:T(8,128)S(1)}, f32[16,128,128]{2,1,0:T(8,128)}, u32[]{:S(2)}) copy-start(f32[16,128,128]{2,1,0:T(8,128)} %get-tuple-element.292) | copy-start | bytes 3145732
  575.8 12.4 %copy-start.3 = (bf16[128,2048]{0,1:T(8,128)(2,1)S(1)}, bf16[128,2048]{0,1:T(8,128)(2,1)}, u32[]{:S(2)}) copy-start(bf16[128,2048]{0,1:T(8,128)(2,1)} %copy-done.2) | copy-start | bytes 1572868
Sparse Core Ops, SparseCore 0:
  15.2 114.0 all-gather.12
  131.4 110.8 all-gather.10
  326.5 90.9 all-reduce.4
  419.1 49.0 all-gather.6
  469.7 49.9 all-gather.8
where the time goes:
time: 600 us; the launch traced here: 597 us
  waiting for transfers between devices  314 us (52%)
  blocking collectives  94.4 us (16%)
  other arithmetic  75.7 us (13%)
  loops' own time  44.9 us (7%)
  matrix products  29.5 us (5%)
  local copies, waits for them, and re-layouts  24.9 us (4%)
  between operations  14.2 us (2%)
    all_gather x4, waiting for transfers between devices, prefix_2(): pieces = jax.tree.map(lambda part: lax.all_gather(part, axis), value)  222 us
    psum x1, waiting for transfers between devices, from_root(): return lax.psum(jnp.where(mine, shard, jnp.zeros_like(shard)), axis)  91.1 us
    select_n x22, other arithmetic, hop(): jnp.where(position < mine, new, old)  67.1 us
    unnamed x2, blocking collectives  55 us
    another operation x2, loops' own time, prefix_2(): return lax.fori_loop(0, count - 1, hop, running)  44.9 us
    psum x1, blocking collectives, from_root(): return lax.psum(jnp.where(mine, shard, jnp.zeros_like(shard)), axis)  39.4 us
    dynamic_slice x22, local copies, waits for them, and re-layouts, hop(): longer = join(running, jax.tree.map(lambda part: part[position], pieces))  14.3 us
  transfers between devices with their start and end apart: 5, of which 4 were waited for; matrix products, arithmetic and copies ran while one was open for 2% of the time, Pallas kernels for 0%

commit v1 on v0

v1 whole, which is shorter than its diff:
```python
import jax
import jax.numpy as jnp
from jax import lax
from jax.experimental import pallas as pl
from jax.experimental.pallas import tpu as pltpu
from jax.sharding import PartitionSpec as P

CG_ITERS = 3
HEADS = 16
WIDTH = 128
ROWS = 128
HALF = ROWS // 2
INFO = 8
PART = HALF + INFO
INNER = 16
OUTER = 8
SIDE = 4
MESH = pl.DeviceIdType.MESH
F32 = jnp.float32
BF16 = jnp.bfloat16


def halves(value):
    high = value.astype(BF16)
    return high, (value - high.astype(F32)).astype(BF16)


def mm(left, right):
    return jnp.dot(left, right, preferred_element_type=F32)


def mm_split(value, stacked):
    return mm(jnp.concatenate(halves(value), 1), stacked)


def twice(value):
    return jnp.concatenate([value, value], 0)


def kernel(
    q_ref,
    k_ref,
    v_ref,
    seg_ref,
    ridge_ref,
    out_ref,
    key_t,
    scales,
    send_g,
    recv_g,
    send_c,
    recv_c,
    total_g,
    early_g,
    total_c,
    early_c,
    back_g,
    prefix_g,
    back_c,
    prefix_c,
    solved,
    send_sem,
    recv_sem,
    total_send_sem,
    total_recv_sem,
):
    group, me = lax.axis_index("outer"), lax.axis_index("inner")
    me_z, me_x = me // SIDE, lax.rem(me, SIDE)

    def peer_at(step):
        x = lax.rem(me_x + lax.rem(step, SIDE), SIDE)
        z = lax.rem(me_z + step // SIDE, SIDE)
        return z * SIDE + x

    def group_at(step):
        return lax.rem(group + OUTER + step, OUTER)

    barrier = pltpu.get_barrier_semaphore()

    def greet(step, carry):
        pl.semaphore_signal(barrier, inc=1, device_id=(group, peer_at(step)), device_id_type=MESH)
        return carry

    lax.fori_loop(1, INNER, greet, 0)
    for step in (-2, -1, 1, 2):
        pl.semaphore_signal(barrier, inc=1, device_id=(group_at(step), me), device_id_type=MESH)

    def exchange(kind, source, target, peer):
        return pltpu.make_async_remote_copy(
            src_ref=source.at[peer],
            dst_ref=target.at[me],
            send_sem=send_sem.at[kind, peer],
            recv_sem=recv_sem.at[kind, me],
            device_id=(group, peer),
            device_id_type=MESH,
        )

    def arrival(kind, source, target, peer):
        return pltpu.make_async_remote_copy(
            src_ref=source.at[peer],
            dst_ref=target.at[peer],
            send_sem=send_sem.at[kind, peer],
            recv_sem=recv_sem.at[kind, peer],
            device_id=(group, peer),
            device_id_type=MESH,
        )

    def start_all(kind, source, target):
        def body(step, carry):
            exchange(kind, source, target, peer_at(step)).start()
            return carry

        lax.fori_loop(1, INNER, body, 0)
        target[me] = source[me]

    def wait_recv_all(kind, source, target):
        def body(step, carry):
            arrival(kind, source, target, peer_at(step)).wait_recv()
            return carry

        lax.fori_loop(1, INNER, body, 0)

    def wait_send_all(kind, source, target):
        def body(step, carry):
            arrival(kind, source, target, peer_at(step)).wait_send()
            return carry

        lax.fori_loop(1, INNER, body, 0)

    def pass_on(kind, source, target, step):
        return pltpu.make_async_remote_copy(
            src_ref=source,
            dst_ref=target.at[step - 1],
            send_sem=total_send_sem.at[kind, step - 1],
            recv_sem=total_recv_sem.at[kind, step - 1],
            device_id=(group_at(step), me),
            device_id_type=MESH,
        )

    row = lax.broadcasted_iota(jnp.int32, (ROWS, ROWS), 0)
    col = lax.broadcasted_iota(jnp.int32, (ROWS, ROWS), 1)
    info_row = lax.broadcasted_iota(jnp.int32, (INFO, WIDTH), 0)
    seg_cols = jnp.broadcast_to(seg_ref[...].astype(F32), (ROWS, ROWS))
    seg_rows = seg_cols.T
    first, last = seg_rows[0:1], seg_rows[ROWS - 1 :]
    weight = (seg_cols[0:1] == last).astype(F32)
    within = jnp.logical_and(row >= col, seg_rows == seg_cols).astype(F32)
    carried = (seg_rows == first).astype(F32)
    ids = jnp.where(info_row == 1, last, jnp.where(info_row == 2, first, 0.0))

    def head_slice(head):
        return pl.ds(pl.multiple_of(head * WIDTH, WIDTH), WIDTH)

    def gram(head):
        keys = k_ref[:, head_slice(head)]
        turned = keys.astype(F32).T
        scale = lax.rsqrt(jnp.sum(turned * turned, 0, keepdims=True) + 1e-06)
        key_t[head] = turned.astype(BF16)
        scales[head] = jnp.broadcast_to(scale, (INFO, WIDTH))
        return mm_split(turned * (weight * scale * scale), twice(keys))

    def gram_pair(pair, carry):
        one, two = gram(2 * pair), gram(2 * pair + 1)
        joined = jnp.where(row <= col, one, two)
        diagonal = jnp.sum(jnp.where(row == col, two, 0.0), 0, keepdims=True)
        info = jnp.where(info_row == 0, diagonal, ids)
        send_g[2 * pair, 0:HALF] = joined[0:HALF]
        send_g[2 * pair + 1, 0:HALF] = joined[HALF:]
        send_g[2 * pair, HALF:PART] = info
        send_g[2 * pair + 1, HALF:PART] = info
        return carry

    lax.fori_loop(0, HEADS // 2, gram_pair, 0, unroll=2)
    pl.semaphore_wait(barrier, INNER - 1 + 4)
    start_all(0, send_g, recv_g)

    def cross(head, carry):
        turned = key_t[head].astype(F32) * (weight * scales[head, 0:1])
        send_c[head] = mm_split(turned, twice(v_ref[:, head_slice(head)]))
        return carry

    lax.fori_loop(0, HEADS, cross, 0, unroll=4)
    start_all(1, send_c, recv_c)

    def last_of(shard):
        return recv_g[shard, HALF + 1 : HALF + 2]

    def first_of(shard):
        return recv_g[shard, HALF + 2 : HALF + 3]

    def total_of(received):
        final = last_of(INNER - 1)

        def body(shard, acc):
            return acc + jnp.where(last_of(shard) == final, received[shard], 0.0)

        return lax.fori_loop(0, INNER - 1, body, received[INNER - 1])

    has_one = (jnp.zeros((1, WIDTH), jnp.int32) + group) >= 1
    has_two = (jnp.zeros((1, WIDTH), jnp.int32) + group) >= 2

    def early_last(which):
        return early_g[which, HALF + 1 : HALF + 2]

    def prefixes(received, early, back):
        start_last = jnp.where(has_one, early_last(0), -1.0)
        second = jnp.where(
            jnp.logical_and(has_two, early_last(1) == start_last), early[1], 0.0
        )
        running = jnp.where(has_one, early[0], 0.0) + second

        def body(shard, carry):
            running, running_last = carry
            back[shard] = jnp.where(running_last == first_of(shard), running, 0.0)
            own_last = last_of(shard)
            return (
                received[shard] + jnp.where(running_last == own_last, running, 0.0),
                own_last,
            )

        lax.fori_loop(0, INNER, body, (running, start_last))

    wait_recv_all(0, send_g, recv_g)
    summed = total_of(recv_g)
    total_g[0:HALF] = summed[0:HALF]
    total_g[HALF:PART] = jnp.where(
        info_row == 0, summed[HALF:PART], recv_g[INNER - 1, HALF:PART]
    )
    for step in (1, 2):
        pass_on(0, total_g, early_g, step).start()
    for step in (1, 2):
        pass_on(0, total_g, early_g, step).wait_recv()
    prefixes(recv_g, early_g, back_g)
    start_all(2, back_g, prefix_g)

    wait_recv_all(1, send_c, recv_c)
    total_c[...] = total_of(recv_c)
    for step in (1, 2):
        pass_on(1, total_c, early_c, step).start()
    for step in (1, 2):
        pass_on(1, total_c, early_c, step).wait_recv()
    prefixes(recv_c, early_c, back_c)
    start_all(3, back_c, prefix_c)

    wait_recv_all(2, back_g, prefix_g)

    def solve(head, gram_in):
        cols = head_slice(head)
        keys, turned = k_ref[:, cols], key_t[head]
        scale = scales[head, 0:1]
        ridge = ridge_ref[head]
        gram_high, gram_low = halves(gram_in)
        both = twice(jnp.concatenate([gram_high, turned], 1))
        key_pair = twice(keys)
        key_mask = within * (scale * scale)
        query = q_ref[:, cols].astype(F32)
        remain = query * lax.rsqrt(jnp.sum(query * query, -1, keepdims=True) + 1e-06)
        search = remain
        remain_square = jnp.sum(remain * remain, -1, keepdims=True)
        answer = jnp.zeros_like(remain)
        for step in range(CG_ITERS):
            high, low = halves(search)
            product = mm(jnp.concatenate([high, low], 1), both)
            from_state = product[:, :WIDTH] + mm(high, gram_low)
            local = mm_split(product[:, WIDTH:] * key_mask, key_pair)
            applied = from_state * carried + local + ridge * search
            stepsize = remain_square / jnp.sum(search * applied, -1, keepdims=True)
            answer = answer + stepsize * search
            if step < CG_ITERS - 1:
                remain = remain - stepsize * applied
                next_square = jnp.sum(remain * remain, -1, keepdims=True)
                search = remain + next_square / remain_square * search
                remain_square = next_square
        scores = mm_split(answer, twice(turned)) * (within * scale)
        out_ref[:, cols] = mm_split(scores, twice(v_ref[:, cols]))
        solved[head] = answer * carried

    def solve_pair(pair, carry):
        joined = jnp.concatenate([prefix_g[2 * pair, 0:HALF], prefix_g[2 * pair + 1, 0:HALF]], 0)
        turned = joined.T
        diagonal = prefix_g[2 * pair, HALF : HALF + 1]
        one = jnp.where(row <= col, joined, turned)
        two = jnp.where(row == col, diagonal, jnp.where(row > col, joined, turned))
        solve(2 * pair, one)
        solve(2 * pair + 1, two)
        return carry

    lax.fori_loop(0, HEADS // 2, solve_pair, 0, unroll=2)

    wait_recv_all(3, back_c, prefix_c)

    def finish(head, carry):
        cols = head_slice(head)
        high, low = halves(solved[head])
        cross_high, cross_low = halves(prefix_c[head])
        out_ref[:, cols] = (
            out_ref[:, cols]
            + mm(jnp.concatenate([high, low], 1), twice(cross_high))
            + mm(high, cross_low)
        )
        return carry

    lax.fori_loop(0, HEADS, finish, 0, unroll=4)

    wait_send_all(0, send_g, recv_g)
    wait_send_all(1, send_c, recv_c)
    wait_send_all(2, back_g, prefix_g)
    wait_send_all(3, back_c, prefix_c)
    for step in (1, 2):
        pass_on(0, total_g, early_g, step).wait_send()
        pass_on(1, total_c, early_c, step).wait_send()


def on_device(queries, key_vectors, value_vectors, segment_ids, ridge_weight):
    vmem = pl.BlockSpec(memory_space=pltpu.VMEM)
    state_g = pltpu.VMEM((INNER, PART, WIDTH), F32)
    state_c = pltpu.VMEM((INNER, ROWS, WIDTH), F32)
    return pl.pallas_call(
        kernel,
        name="mesa",
        out_shape=jax.ShapeDtypeStruct((ROWS, HEADS * WIDTH), F32),
        in_specs=[vmem, vmem, vmem, vmem, pl.BlockSpec(memory_space=pltpu.SMEM)],
        out_specs=vmem,
        scratch_shapes=[
            pltpu.VMEM((HEADS, WIDTH, ROWS), BF16),
            pltpu.VMEM((HEADS, INFO, WIDTH), F32),
            state_g,
            state_g,
            state_c,
            state_c,
            pltpu.VMEM((PART, WIDTH), F32),
            pltpu.VMEM((2, PART, WIDTH), F32),
            pltpu.VMEM((ROWS, WIDTH), F32),
            pltpu.VMEM((2, ROWS, WIDTH), F32),
            state_g,
            state_g,
            state_c,
            state_c,
            pltpu.VMEM((HEADS, ROWS, WIDTH), F32),
            pltpu.SemaphoreType.DMA((4, INNER)),
            pltpu.SemaphoreType.DMA((4, INNER)),
            pltpu.SemaphoreType.DMA((2, 2)),
            pltpu.SemaphoreType.DMA((2, 2)),
        ],
        compiler_params=pltpu.CompilerParams(
            collective_id=0, has_side_effects=True, vmem_limit_bytes=48 << 20
        ),
    )(
        queries,
        key_vectors,
        value_vectors,
        segment_ids.reshape(1, ROWS),
        ridge_weight,
    )


def solution(mesh):
    spec = P(("outer", "inner"), None)
    return jax.shard_map(
        on_device,
        mesh=mesh,
        in_specs=(spec, spec, spec, P(("outer", "inner")), P()),
        out_specs=spec,
        check_vma=False,
    )
```

time: 600 us -> 65.7 us (0.11)
  waiting for transfers between devices: 314 us -> 0 us
  blocking collectives: 94.4 us -> 0 us
  other arithmetic: 75.7 us -> 0 us
  Pallas kernels: 0 us -> 59.9 us
  loops' own time: 44.9 us -> 0 us
  matrix products: 29.5 us -> 0 us
  local copies, waits for them, and re-layouts: 24.9 us -> 4.77 us
  between operations: 14.2 us -> 0.01 us
    all_gather x4 -> x0, waiting for transfers between devices: 222 us -> none  [prefix_2(): pieces = jax.tree.map(lambda part: lax.all_gather(part, axis), value)]
    psum x1 -> x0, waiting for transfers between devices: 91.1 us -> none  [from_root(): return lax.psum(jnp.where(mine, shard, jnp.zeros_like(shard)), axis)]
    select_n x22 -> x0, other arithmetic: 67.1 us -> none  [hop(): jnp.where(position < mine, new, old)]
    pallas_call x0 -> x1, Pallas kernels: none -> 59.9 us  [on_device(): pl.pallas_call(kernel, name='mesa', out_shape=jax.ShapeDtypeStruct((ROWS,...]
    unnamed x2 -> x0, blocking collectives: 55 us -> none
    another operation x2 -> x0, loops' own time: 44.9 us -> none  [prefix_2(): return lax.fori_loop(0, count - 1, hop, running)]
    psum x1 -> x0, blocking collectives: 39.4 us -> none  [from_root(): return lax.psum(jnp.where(mine, shard, jnp.zeros_like(shard)), axis)]
    dot_general x14 -> x0, matrix products: 29.5 us -> none  [the longest x3 8.63 us: span_solve(): jnp.einsum('hts,hse->hte', apply_scores, key_rows, precision=highest)]
  transfers between devices with their start and end apart: 5 -> 0, of which waited for: 4 -> 0; matrix products, arithmetic and copies ran while one was open for 2% -> 0% of each run, Pallas kernels for 0% -> 0%
where the time goes in v1:
time: 65.7 us; the launch traced here: 64.6 us
  Pallas kernels  59.9 us (91%)
  local copies, waits for them, and re-layouts  4.77 us (7%)
    pallas_call x1, Pallas kernels, on_device(): pl.pallas_call(kernel, name='mesa', out_shape=jax.ShapeDtypeStruct((ROWS,...  59.9 us
    unnamed x11, local copies, waits for them, and re-layouts  4.77 us

profile of v1, /device:TPU:0, one launch (start us, length us, event | category | flops | bytes accessed | tf_op | source)
XLA Modules:
  0.0 64.6 jit_solution(4751773928143425165)
XLA Ops:
  0.0 0.0 copy-start.4
  0.0 0.0 copy-start.3
  0.0 0.7 %copy-done.4 = f32[16]{0:T(128)S(1)} copy-done((f32[16]{0:T(128)S(1)}, f32[16]{0:T(128)}, u32[]{:S(2)}) %copy-start.4) | copy-done | bytes 88
  0.7 0.0 copy-done.3
  0.7 0.0 copy-start
  0.7 1.0 %copy-done = bf16[128,2048]{1,0:T(8,128)(2,1)S(1)} copy-done((bf16[128,2048]{1,0:T(8,128)(2,1)S(1)}, bf16[128,2048]{1,0:T(8,128)(2,1)}, u32[]{:S(2)}) %copy-start) | copy-done | bytes 524312
  1.7 0.0 copy-start.1
  1.7 1.0 %copy-done.1 = bf16[128,2048]{1,0:T(8,128)(2,1)S(1)} copy-done((bf16[128,2048]{1,0:T(8,128)(2,1)S(1)}, bf16[128,2048]{1,0:T(8,128)(2,1)}, u32[]{:S(2)}) %copy-start.1) | copy-done | bytes 524312
  2.8 0.0 copy-start.2
  2.8 1.0 %copy-done.2 = bf16[128,2048]{1,0:T(8,128)(2,1)S(1)} copy-done((bf16[128,2048]{1,0:T(8,128)(2,1)S(1)}, bf16[128,2048]{1,0:T(8,128)(2,1)}, u32[]{:S(2)}) %copy-start.2) | copy-done | bytes 524312
  3.8 59.9 %mesa.1 = f32[128,2048]{1,0:T(8,128)S(1)} custom-call(bf16[128,2048]{1,0:T(8,128)(2,1)S(1)} %copy-done, bf16[128,2048]{1,0:T(8,128)(2,1)S(1)} %copy-done.1, bf16[128,2048]{1,0:T(8,128)(2,1)S(1)} %copy-done.2, s32[1,128]{1,0:T(1,128)S(1)} %bitcast.1, f32[16]{0:T(128)S(1)} %copy-done.4), custom_call_target="tpu_custom_call" | custom-call | tf_op jit(solution)/shard_map/mesa/pallas_call | solution.py:318
  63.7 1.0 %copy.7 = f32[128,2048]{1,0:T(8,128)} copy(f32[128,2048]{1,0:T(8,128)S(1)} %mesa.1) | data formatting | bytes 2097152
Async XLA Ops:
  0.0 0.7 %copy-start.4 = (f32[16]{0:T(128)S(1)}, f32[16]{0:T(128)}, u32[]{:S(2)}) copy-start(f32[16]{0:T(128)} %ridge_ref.1) | copy-start | bytes 196
  0.0 0.7 %copy-start.3 = (s32[128]{0:T(128)S(1)}, s32[128]{0:T(128)}, u32[]{:S(2)}) copy-start(s32[128]{0:T(128)} %param.8) | copy-start | bytes 1540
  0.7 1.0 %copy-start = (bf16[128,2048]{1,0:T(8,128)(2,1)S(1)}, bf16[128,2048]{1,0:T(8,128)(2,1)}, u32[]{:S(2)}) copy-start(bf16[128,2048]{1,0:T(8,128)(2,1)} %q_ref.1) | copy-start | bytes 1572868
  1.7 1.0 %copy-start.1 = (bf16[128,2048]{1,0:T(8,128)(2,1)S(1)}, bf16[128,2048]{1,0:T(8,128)(2,1)}, u32[]{:S(2)}) copy-start(bf16[128,2048]{1,0:T(8,128)(2,1)} %k_ref.1) | copy-start | bytes 1572868
  2.8 1.0 %copy-start.2 = (bf16[128,2048]{1,0:T(8,128)(2,1)S(1)}, bf16[128,2048]{1,0:T(8,128)(2,1)}, u32[]{:S(2)}) copy-start(bf16[128,2048]{1,0:T(8,128)(2,1)} %v_ref.1) | copy-start | bytes 1572868

commit v2 on v1

v2 whole, which is shorter than its diff:
```python
import jax
import jax.numpy as jnp
from jax import lax
from jax.experimental import pallas as pl
from jax.experimental.pallas import tpu as pltpu
from jax.sharding import PartitionSpec as P

CG_ITERS = 3
HEADS = 16
WIDTH = 128
ROWS = 128
HALF = ROWS // 2
INFO = 8
PART = HALF + INFO
INNER = 16
OUTER = 8
SIDE = 4
GROUP = 4
OFFSETS = sorted(
    ((x, z) for z in range(SIDE) for x in range(SIDE) if (x, z) != (0, 0)),
    key=lambda o: -(min(o[0], SIDE - o[0]) + min(o[1], SIDE - o[1])),
)
MESH = pl.DeviceIdType.MESH
F32 = jnp.float32
BF16 = jnp.bfloat16


def halves(value):
    high = value.astype(BF16)
    return high, (value - high.astype(F32)).astype(BF16)


def mm(left, right):
    return jnp.dot(left, right, preferred_element_type=F32)


def mm_split(value, stacked):
    return mm(jnp.concatenate(halves(value), 1), stacked)


def twice(value):
    return jnp.concatenate([value, value], 0)


def twice_wide(value):
    return jnp.concatenate([value, value], 1)


def kernel(
    q_hbm,
    k_hbm,
    v_hbm,
    seg_ref,
    ridge_ref,
    out_ref,
    q_ref,
    k_ref,
    v_ref,
    key_t,
    scales,
    masks,
    query_t,
    first_local,
    send_g,
    recv_g,
    send_c,
    recv_c,
    total_g,
    early_g,
    total_c,
    early_c,
    back_g,
    prefix_g,
    back_c,
    prefix_c,
    solved,
    load_sem,
    send_sem,
    recv_sem,
    total_send_sem,
    total_recv_sem,
):
    group, me = lax.axis_index("outer"), lax.axis_index("inner")
    me_z, me_x = me // SIDE, lax.rem(me, SIDE)
    peers = [
        lax.rem(me_z + z, SIDE) * SIDE + lax.rem(me_x + x, SIDE) for x, z in OFFSETS
    ]

    def group_at(step):
        return lax.rem(group + OUTER + step, OUTER)

    loads = [
        pltpu.make_async_copy(source, target, load_sem.at[place])
        for place, (source, target) in enumerate(
            ((k_hbm, k_ref), (v_hbm, v_ref), (q_hbm, q_ref))
        )
    ]
    for load in loads:
        load.start()

    barrier = pltpu.get_barrier_semaphore()
    for peer in peers:
        pl.semaphore_signal(barrier, inc=1, device_id=(group, peer), device_id_type=MESH)
    for step in (-2, -1, 1, 2):
        pl.semaphore_signal(barrier, inc=1, device_id=(group_at(step), me), device_id_type=MESH)

    def start_all(kind, source, target, rows):
        for peer in peers:
            pltpu.make_async_remote_copy(
                src_ref=source.at[peer, rows],
                dst_ref=target.at[me, rows],
                send_sem=send_sem.at[kind],
                recv_sem=recv_sem.at[kind],
                device_id=(group, peer),
                device_id_type=MESH,
            ).start()
        target[me, rows] = source[me, rows]

    def all_of(kind, source, target, rows):
        blocks = pl.ds(0, INNER - 1)
        return pltpu.make_async_remote_copy(
            src_ref=source.at[blocks, rows],
            dst_ref=target.at[blocks, rows],
            send_sem=send_sem.at[kind],
            recv_sem=recv_sem.at[kind],
            device_id=(group, peers[0]),
            device_id_type=MESH,
        )

    def pass_on(kind, source, target, step, rows):
        return pltpu.make_async_remote_copy(
            src_ref=source.at[rows],
            dst_ref=target.at[step - 1, rows],
            send_sem=total_send_sem.at[kind, step - 1],
            recv_sem=total_recv_sem.at[kind, step - 1],
            device_id=(group_at(step), me),
            device_id_type=MESH,
        )

    row = lax.broadcasted_iota(jnp.int32, (ROWS, ROWS), 0)
    col = lax.broadcasted_iota(jnp.int32, (ROWS, ROWS), 1)
    info_row = lax.broadcasted_iota(jnp.int32, (INFO, WIDTH), 0)
    seg_cols = jnp.broadcast_to(seg_ref[...].astype(F32), (ROWS, ROWS))
    seg_rows = seg_cols.T
    first, last = seg_rows[0:1], seg_rows[ROWS - 1 :]
    weight = (seg_cols[0:1] == last).astype(F32)
    same = seg_rows == seg_cols
    within = jnp.logical_and(row >= col, same).astype(F32)
    within_t = jnp.logical_and(col >= row, same).astype(F32)
    carried_t = (seg_cols[0:1] == first).astype(F32)
    ids = jnp.where(info_row == 1, last, jnp.where(info_row == 2, first, 0.0))
    whole, lower, upper = pl.ds(0, PART), pl.ds(0, HALF), pl.ds(HALF, HALF)

    def head_slice(head):
        return pl.ds(pl.multiple_of(head * WIDTH, WIDTH), WIDTH)

    def gram(head):
        keys = k_ref[:, head_slice(head)]
        turned = keys.astype(F32).T
        scale = lax.rsqrt(jnp.sum(turned * turned, 0, keepdims=True) + 1e-06)
        key_t[head] = turned.astype(BF16)
        scales[head] = jnp.broadcast_to(scale, (INFO, WIDTH))
        return mm_split(turned * (weight * scale * scale), twice(keys))

    def gram_pair(pair, carry):
        one, two = gram(2 * pair), gram(2 * pair + 1)
        joined = jnp.where(row <= col, one, two)
        diagonal = jnp.sum(jnp.where(row == col, two, 0.0), 0, keepdims=True)
        info = jnp.where(info_row == 0, diagonal, ids)
        send_g[2 * pair, 0:HALF] = joined[0:HALF]
        send_g[2 * pair + 1, 0:HALF] = joined[HALF:]
        send_g[2 * pair, HALF:PART] = info
        send_g[2 * pair + 1, HALF:PART] = info
        return carry

    loads[0].wait()
    lax.fori_loop(0, HEADS // 2, gram_pair, 0, unroll=2)
    pl.semaphore_wait(barrier, INNER - 1 + 4)
    start_all(0, send_g, recv_g, whole)

    def cross(head, carry):
        turned = key_t[head].astype(F32) * (weight * scales[head, 0:1])
        send_c[head] = mm_split(turned, twice(v_ref[:, head_slice(head)]))
        return carry

    loads[1].wait()
    lax.fori_loop(0, HEADS, cross, 0, unroll=4)
    start_all(1, send_c, recv_c, lower)
    start_all(2, send_c, recv_c, upper)

    def prepare(head, carry):
        cols = head_slice(head)
        keys = k_ref[:, cols]
        widened = keys.astype(F32)
        scale = lax.rsqrt(jnp.sum(widened * widened, -1, keepdims=True) + 1e-06)
        mask = within_t * (scale * scale)
        masks[head] = mask
        query = q_ref[:, cols].astype(F32).T
        query = query * lax.rsqrt(jnp.sum(query * query, 0, keepdims=True) + 1e-06)
        query_t[head] = query
        scores = mm(twice_wide(keys), jnp.concatenate(halves(query), 0)) * mask
        local = mm(twice_wide(key_t[head]), jnp.concatenate(halves(scores), 0))
        first_local[head] = local + ridge_ref[head] * query
        return carry

    loads[2].wait()
    lax.fori_loop(0, HEADS, prepare, 0, unroll=4)

    def last_of(shard):
        return recv_g[shard, HALF + 1 : HALF + 2]

    def first_of(shard):
        return recv_g[shard, HALF + 2 : HALF + 3]

    def total_of(received, rows):
        final = last_of(INNER - 1)
        summed = received[INNER - 1, rows]
        for shard in range(INNER - 1):
            summed = summed + jnp.where(last_of(shard) == final, received[shard, rows], 0.0)
        return summed

    has_one = (jnp.zeros((1, WIDTH), jnp.int32) + group) >= 1
    has_two = (jnp.zeros((1, WIDTH), jnp.int32) + group) >= 2

    def early_last(which):
        return early_g[which, HALF + 1 : HALF + 2]

    def prefixes(received, early, back, rows):
        running_last = jnp.where(has_one, early_last(0), -1.0)
        second = jnp.where(
            jnp.logical_and(has_two, early_last(1) == running_last), early[1, rows], 0.0
        )
        running = jnp.where(has_one, early[0, rows], 0.0) + second
        for shard in range(INNER):
            back[shard, rows] = jnp.where(running_last == first_of(shard), running, 0.0)
            own_last = last_of(shard)
            running = received[shard, rows] + jnp.where(running_last == own_last, running, 0.0)
            running_last = own_last

    def hand_on(kind, source, target, rows):
        for step in (1, 2):
            pass_on(kind, source, target, step, rows).start()

    def take(kind, source, target, rows):
        for step in (1, 2):
            pass_on(kind, source, target, step, rows).wait_recv()

    all_of(0, send_g, recv_g, whole).wait_recv()
    summed = total_of(recv_g, whole)
    total_g[0:HALF] = summed[0:HALF]
    total_g[HALF:PART] = jnp.where(
        info_row == 0, summed[HALF:PART], recv_g[INNER - 1, HALF:PART]
    )
    hand_on(0, total_g, early_g, whole)
    take(0, total_g, early_g, whole)
    prefixes(recv_g, early_g, back_g, whole)
    start_all(3, back_g, prefix_g, whole)

    for kind, rows in ((1, lower), (2, upper)):
        all_of(kind, send_c, recv_c, rows).wait_recv()
        total_c[rows] = total_of(recv_c, rows)
        hand_on(kind, total_c, early_c, rows)
        take(kind, total_c, early_c, rows)
        prefixes(recv_c, early_c, back_c, rows)
        start_all(kind + 3, back_c, prefix_c, rows)

    all_of(3, back_g, prefix_g, whole).wait_recv()

    def solve(heads, grams):
        mats, pairs, searches, remains, squares, answers = [], [], [], [], [], []
        for head, gram_in in zip(heads, grams):
            keys = k_ref[:, head_slice(head)]
            mats.append(twice_wide(jnp.concatenate([*halves(gram_in), keys], 0)))
            pairs.append(twice_wide(key_t[head]))
            query = query_t[head]
            searches.append(query)
            remains.append(query)
            squares.append(jnp.sum(query * query, 0, keepdims=True))
            answers.append(None)
        count = range(len(heads))
        for step in range(CG_ITERS):
            stacks = [jnp.concatenate(halves(searches[n]), 0) for n in count]
            if step == 0:
                products = [mm(mats[n][: 2 * WIDTH], stacks[n]) for n in count]
                locals_ = [first_local[heads[n]] for n in count]
            else:
                products = [mm(mats[n], stacks[n]) for n in count]
                scores = [products[n][2 * WIDTH :] * masks[heads[n]] for n in count]
                locals_ = [
                    mm(pairs[n], jnp.concatenate(halves(scores[n]), 0))
                    + ridge_ref[heads[n]] * searches[n]
                    for n in count
                ]
            applied = [
                (products[n][:WIDTH] + products[n][WIDTH : 2 * WIDTH]) * carried_t + locals_[n]
                for n in count
            ]
            sizes = [
                squares[n] / jnp.sum(searches[n] * applied[n], 0, keepdims=True) for n in count
            ]
            for n in count:
                move = sizes[n] * searches[n]
                answers[n] = move if step == 0 else answers[n] + move
            if step < CG_ITERS - 1:
                remains = [remains[n] - sizes[n] * applied[n] for n in count]
                nexts = [jnp.sum(remains[n] * remains[n], 0, keepdims=True) for n in count]
                searches = [
                    remains[n] + (nexts[n] / squares[n]) * searches[n] for n in count
                ]
                squares = nexts
        for n in count:
            head = heads[n]
            solved[head] = answers[n].T

    def solve_some(some, carry):
        heads, grams = [], []
        for offset in range(GROUP // 2):
            pair = some * (GROUP // 2) + offset
            joined = jnp.concatenate(
                [prefix_g[2 * pair, 0:HALF], prefix_g[2 * pair + 1, 0:HALF]], 0
            )
            turned = joined.T
            diagonal = prefix_g[2 * pair, HALF : HALF + 1]
            grams.append(jnp.where(row <= col, joined, turned))
            grams.append(
                jnp.where(row == col, diagonal, jnp.where(row > col, joined, turned))
            )
            heads += [2 * pair, 2 * pair + 1]
        solve(heads, grams)
        return carry

    lax.fori_loop(0, HEADS // GROUP, solve_some, 0)

    def read_out(head, carry):
        cols = head_slice(head)
        scale = scales[head, 0:1]
        scores = mm_split(solved[head], twice(key_t[head])) * (within * scale)
        out_ref[:, cols] = mm_split(scores, twice(v_ref[:, cols]))
        return carry

    lax.fori_loop(0, HEADS, read_out, 0, unroll=4)
    carried = (seg_rows == first).astype(F32)

    def add_cross(rows):
        def body(head, carry):
            cols = head_slice(head)
            high, low = halves(solved[head] * carried)
            high, low = high[:, rows.start : rows.start + HALF], low[:, rows.start : rows.start + HALF]
            cross_high, cross_low = halves(prefix_c[head, rows])
            stacked = jnp.concatenate([cross_high, cross_high, cross_low], 0)
            out_ref[:, cols] = out_ref[:, cols] + mm(
                jnp.concatenate([high, low, high], 1), stacked
            )
            return carry

        lax.fori_loop(0, HEADS, body, 0, unroll=4)

    all_of(0, send_g, recv_g, whole).wait_send()
    for kind, rows in ((1, lower), (2, upper)):
        all_of(kind, send_c, recv_c, rows).wait_send()
    all_of(3, back_g, prefix_g, whole).wait_send()
    for step in (1, 2):
        pass_on(0, total_g, early_g, step, whole).wait_send()
        pass_on(1, total_c, early_c, step, lower).wait_send()
        pass_on(2, total_c, early_c, step, upper).wait_send()
    all_of(4, back_c, prefix_c, lower).wait_recv()
    add_cross(lower)
    all_of(4, back_c, prefix_c, lower).wait_send()
    all_of(5, back_c, prefix_c, upper).wait_recv()
    add_cross(upper)
    all_of(5, back_c, prefix_c, upper).wait_send()


def on_device(queries, key_vectors, value_vectors, segment_ids, ridge_weight):
    vmem = pl.BlockSpec(memory_space=pltpu.VMEM)
    hbm = pl.BlockSpec(memory_space=pltpu.HBM)
    operand = pltpu.VMEM((ROWS, HEADS * WIDTH), BF16)
    state_g = pltpu.VMEM((INNER, PART, WIDTH), F32)
    state_c = pltpu.VMEM((INNER, ROWS, WIDTH), F32)
    return pl.pallas_call(
        kernel,
        name="mesa",
        out_shape=jax.ShapeDtypeStruct((ROWS, HEADS * WIDTH), F32),
        in_specs=[hbm, hbm, hbm, vmem, pl.BlockSpec(memory_space=pltpu.SMEM)],
        out_specs=vmem,
        scratch_shapes=[
            operand,
            operand,
            operand,
            pltpu.VMEM((HEADS, WIDTH, ROWS), BF16),
            pltpu.VMEM((HEADS, INFO, WIDTH), F32),
            state_c,
            state_c,
            state_c,
            state_g,
            state_g,
            state_c,
            state_c,
            pltpu.VMEM((PART, WIDTH), F32),
            pltpu.VMEM((2, PART, WIDTH), F32),
            pltpu.VMEM((ROWS, WIDTH), F32),
            pltpu.VMEM((2, ROWS, WIDTH), F32),
            state_g,
            state_g,
            state_c,
            state_c,
            state_c,
            pltpu.SemaphoreType.DMA((3,)),
            pltpu.SemaphoreType.DMA((6,)),
            pltpu.SemaphoreType.DMA((6,)),
            pltpu.SemaphoreType.DMA((3, 2)),
            pltpu.SemaphoreType.DMA((3, 2)),
        ],
        compiler_params=pltpu.CompilerParams(
            collective_id=0, has_side_effects=True, vmem_limit_bytes=48 << 20
        ),
    )(
        queries,
        key_vectors,
        value_vectors,
        segment_ids.reshape(1, ROWS),
        ridge_weight,
    )


def solution(mesh):
    spec = P(("outer", "inner"), None)
    return jax.shard_map(
        on_device,
        mesh=mesh,
        in_specs=(spec, spec, spec, P(("outer", "inner")), P()),
        out_specs=spec,
        check_vma=False,
    )
```

time: 65.7 us -> 53 us (0.81)
  Pallas kernels: 59.9 us -> 47.3 us
    pallas_call x1, Pallas kernels: 59.9 us -> 47.3 us  [on_device(): pl.pallas_call(kernel, name='mesa', out_shape=jax.ShapeDtypeStruct((ROWS,...]
where the time goes in v2:
time: 53 us; the launch traced here: 52.1 us
  Pallas kernels  47.3 us (89%)
  local copies, waits for them, and re-layouts  4.77 us (9%)
    pallas_call x1, Pallas kernels, on_device(): pl.pallas_call(kernel, name='mesa', out_shape=jax.ShapeDtypeStruct((ROWS,...  47.3 us
    unnamed x11, local copies, waits for them, and re-layouts  4.77 us

profile of v2, /device:TPU:0, one launch (start us, length us, event | category | flops | bytes accessed | tf_op | source)
XLA Modules:
  0.0 52.1 jit_solution(3049111118109182840)
XLA Ops:
  0.0 0.0 copy-start.4
  0.0 0.0 copy-start.3
  0.0 0.7 %copy-done.4 = f32[16]{0:T(128)S(1)} copy-done((f32[16]{0:T(128)S(1)}, f32[16]{0:T(128)}, u32[]{:S(2)}) %copy-start.4) | copy-done | bytes 88
  0.7 0.0 copy-done.3
  0.7 0.0 copy-start
  0.7 1.0 %copy-done = bf16[128,2048]{1,0:T(8,128)(2,1)S(1)} copy-done((bf16[128,2048]{1,0:T(8,128)(2,1)S(1)}, bf16[128,2048]{1,0:T(8,128)(2,1)}, u32[]{:S(2)}) %copy-start) | copy-done | bytes 524312
  1.7 0.0 copy-start.1
  1.7 1.0 %copy-done.1 = bf16[128,2048]{1,0:T(8,128)(2,1)S(1)} copy-done((bf16[128,2048]{1,0:T(8,128)(2,1)S(1)}, bf16[128,2048]{1,0:T(8,128)(2,1)}, u32[]{:S(2)}) %copy-start.1) | copy-done | bytes 524312
  2.8 0.0 copy-start.2
  2.8 1.0 %copy-done.2 = bf16[128,2048]{1,0:T(8,128)(2,1)S(1)} copy-done((bf16[128,2048]{1,0:T(8,128)(2,1)S(1)}, bf16[128,2048]{1,0:T(8,128)(2,1)}, u32[]{:S(2)}) %copy-start.2) | copy-done | bytes 524312
  3.8 47.3 %mesa.1 = f32[128,2048]{1,0:T(8,128)S(1)} custom-call(bf16[128,2048]{1,0:T(8,128)(2,1)S(1)} %copy-done, bf16[128,2048]{1,0:T(8,128)(2,1)S(1)} %copy-done.1, bf16[128,2048]{1,0:T(8,128)(2,1)S(1)} %copy-done.2, s32[1,128]{1,0:T(1,128)S(1)} %bitcast.1, f32[16]{0:T(128)S(1)} %copy-done.4), custom_call_target="tpu_custom_call" | custom-call | tf_op jit(solution)/shard_map/mesa/pallas_call | solution.py:380
  51.1 1.0 %copy.7 = f32[128,2048]{1,0:T(8,128)} copy(f32[128,2048]{1,0:T(8,128)S(1)} %mesa.1) | data formatting | bytes 2097152
Async XLA Ops:
  0.0 0.7 %copy-start.4 = (f32[16]{0:T(128)S(1)}, f32[16]{0:T(128)}, u32[]{:S(2)}) copy-start(f32[16]{0:T(128)} %ridge_ref.1) | copy-start | bytes 196
  0.0 0.7 %copy-start.3 = (s32[128]{0:T(128)S(1)}, s32[128]{0:T(128)}, u32[]{:S(2)}) copy-start(s32[128]{0:T(128)} %param.8) | copy-start | bytes 1540
  0.7 1.0 %copy-start = (bf16[128,2048]{1,0:T(8,128)(2,1)S(1)}, bf16[128,2048]{1,0:T(8,128)(2,1)}, u32[]{:S(2)}) copy-start(bf16[128,2048]{1,0:T(8,128)(2,1)} %q_hbm.1) | copy-start | bytes 1572868
  1.7 1.0 %copy-start.1 = (bf16[128,2048]{1,0:T(8,128)(2,1)S(1)}, bf16[128,2048]{1,0:T(8,128)(2,1)}, u32[]{:S(2)}) copy-start(bf16[128,2048]{1,0:T(8,128)(2,1)} %k_hbm.1) | copy-start | bytes 1572868
  2.8 1.0 %copy-start.2 = (bf16[128,2048]{1,0:T(8,128)(2,1)S(1)}, bf16[128,2048]{1,0:T(8,128)(2,1)}, u32[]{:S(2)}) copy-start(bf16[128,2048]{1,0:T(8,128)(2,1)} %v_hbm.1) | copy-start | bytes 1572868

commit v3 on v2

--- a/solution.py
+++ b/solution.py
@@ -16,6 +16,7 @@
 OUTER = 8
 SIDE = 4
 GROUP = 4
+LAST = 5
 OFFSETS = sorted(
     ((x, z) for z in range(SIDE) for x in range(SIDE) if (x, z) != (0, 0)),
     key=lambda o: -(min(o[0], SIDE - o[0]) + min(o[1], SIDE - o[1])),
@@ -50,12 +51,14 @@
     q_hbm,
     k_hbm,
     v_hbm,
-    seg_ref,
-    ridge_ref,
+    seg_hbm,
+    ridge_hbm,
     out_ref,
     q_ref,
     k_ref,
     v_ref,
+    seg_ref,
+    ridge_ref,
     key_t,
     scales,
     masks,
@@ -92,7 +95,13 @@
     loads = [
         pltpu.make_async_copy(source, target, load_sem.at[place])
         for place, (source, target) in enumerate(
-            ((k_hbm, k_ref), (v_hbm, v_ref), (q_hbm, q_ref))
+            (
+                (seg_hbm, seg_ref),
+                (k_hbm, k_ref),
+                (v_hbm, v_ref),
+                (q_hbm, q_ref),
+                (ridge_hbm, ridge_ref),
+            )
         )
     ]
     for load in loads:
@@ -104,8 +113,10 @@
     for step in (-2, -1, 1, 2):
         pl.semaphore_signal(barrier, inc=1, device_id=(group_at(step), me), device_id_type=MESH)
 
-    def start_all(kind, source, target, rows):
-        for peer in peers:
+    ranked = [place + (place >= me).astype(jnp.int32) for place in range(INNER - 1)]
+
+    def start_all(kind, source, target, rows, order):
+        for peer in order:
             pltpu.make_async_remote_copy(
                 src_ref=source.at[peer, rows],
                 dst_ref=target.at[me, rows],
@@ -137,6 +148,7 @@
             device_id_type=MESH,
         )
 
+    loads[0].wait()
     row = lax.broadcasted_iota(jnp.int32, (ROWS, ROWS), 0)
     col = lax.broadcasted_iota(jnp.int32, (ROWS, ROWS), 1)
     info_row = lax.broadcasted_iota(jnp.int32, (INFO, WIDTH), 0)
@@ -150,6 +162,8 @@
     carried_t = (seg_cols[0:1] == first).astype(F32)
     ids = jnp.where(info_row == 1, last, jnp.where(info_row == 2, first, 0.0))
     whole, lower, upper = pl.ds(0, PART), pl.ds(0, HALF), pl.ds(HALF, HALF)
+    sent = pl.ds(0, HALF + 3)
+    returned = pl.ds(0, HALF + 1)
 
     def head_slice(head):
         return pl.ds(pl.multiple_of(head * WIDTH, WIDTH), WIDTH)
@@ -173,20 +187,20 @@
         send_g[2 * pair + 1, HALF:PART] = info
         return carry
 
-    loads[0].wait()
+    loads[1].wait()
     lax.fori_loop(0, HEADS // 2, gram_pair, 0, unroll=2)
     pl.semaphore_wait(barrier, INNER - 1 + 4)
-    start_all(0, send_g, recv_g, whole)
+    start_all(0, send_g, recv_g, sent, peers)
 
     def cross(head, carry):
         turned = key_t[head].astype(F32) * (weight * scales[head, 0:1])
         send_c[head] = mm_split(turned, twice(v_ref[:, head_slice(head)]))
         return carry
 
-    loads[1].wait()
+    loads[2].wait()
     lax.fori_loop(0, HEADS, cross, 0, unroll=4)
-    start_all(1, send_c, recv_c, lower)
-    start_all(2, send_c, recv_c, upper)
+    start_all(1, send_c, recv_c, lower, peers)
+    start_all(2, send_c, recv_c, upper, peers)
 
     def prepare(head, carry):
         cols = head_slice(head)
@@ -203,7 +217,8 @@
         first_local[head] = local + ridge_ref[head] * query
         return carry
 
-    loads[2].wait()
+    loads[3].wait()
+    loads[4].wait()
     lax.fori_loop(0, HEADS, prepare, 0, unroll=4)
 
     def last_of(shard):
@@ -245,16 +260,16 @@
         for step in (1, 2):
             pass_on(kind, source, target, step, rows).wait_recv()
 
-    all_of(0, send_g, recv_g, whole).wait_recv()
+    all_of(0, send_g, recv_g, sent).wait_recv()
     summed = total_of(recv_g, whole)
     total_g[0:HALF] = summed[0:HALF]
     total_g[HALF:PART] = jnp.where(
         info_row == 0, summed[HALF:PART], recv_g[INNER - 1, HALF:PART]
     )
-    hand_on(0, total_g, early_g, whole)
-    take(0, total_g, early_g, whole)
+    hand_on(0, total_g, early_g, sent)
+    take(0, total_g, early_g, sent)
     prefixes(recv_g, early_g, back_g, whole)
-    start_all(3, back_g, prefix_g, whole)
+    start_all(3, back_g, prefix_g, returned, peers)
 
     for kind, rows in ((1, lower), (2, upper)):
         all_of(kind, send_c, recv_c, rows).wait_recv()
@@ -262,9 +277,9 @@
         hand_on(kind, total_c, early_c, rows)
         take(kind, total_c, early_c, rows)
         prefixes(recv_c, early_c, back_c, rows)
-        start_all(kind + 3, back_c, prefix_c, rows)
-
-    all_of(3, back_g, prefix_g, whole).wait_recv()
+        start_all(kind + 3, back_c, prefix_c, rows, peers if kind == 1 else peers)
+
+    all_of(3, back_g, prefix_g, returned).wait_recv()
 
     def solve(heads, grams):
         mats, pairs, searches, remains, squares, answers = [], [], [], [], [], []
@@ -341,34 +356,39 @@
     lax.fori_loop(0, HEADS, read_out, 0, unroll=4)
     carried = (seg_rows == first).astype(F32)
 
-    def add_cross(rows):
-        def body(head, carry):
-            cols = head_slice(head)
-            high, low = halves(solved[head] * carried)
-            high, low = high[:, rows.start : rows.start + HALF], low[:, rows.start : rows.start + HALF]
-            cross_high, cross_low = halves(prefix_c[head, rows])
-            stacked = jnp.concatenate([cross_high, cross_high, cross_low], 0)
-            out_ref[:, cols] = out_ref[:, cols] + mm(
-                jnp.concatenate([high, low, high], 1), stacked
-            )
-            return carry
-
-        lax.fori_loop(0, HEADS, body, 0, unroll=4)
-
-    all_of(0, send_g, recv_g, whole).wait_send()
+    def add_cross(head, rows):
+        cols = head_slice(head)
+        answer = solved[head, :, rows.start : rows.start + HALF] * carried[:, :HALF]
+        high, low = halves(answer)
+        cross_high, cross_low = halves(prefix_c[head, rows])
+        out_ref[:, cols] = out_ref[:, cols] + mm(
+            jnp.concatenate([high, low, high], 1),
+            jnp.concatenate([cross_high, cross_high, cross_low], 0),
+        )
+
+    def add_lower(head, carry):
+        add_cross(head, lower)
+        return carry
+
+    all_of(0, send_g, recv_g, sent).wait_send()
     for kind, rows in ((1, lower), (2, upper)):
         all_of(kind, send_c, recv_c, rows).wait_send()
-    all_of(3, back_g, prefix_g, whole).wait_send()
+    all_of(3, back_g, prefix_g, returned).wait_send()
     for step in (1, 2):
-        pass_on(0, total_g, early_g, step, whole).wait_send()
+        pass_on(0, total_g, early_g, step, sent).wait_send()
         pass_on(1, total_c, early_c, step, lower).wait_send()
         pass_on(2, total_c, early_c, step, upper).wait_send()
     all_of(4, back_c, prefix_c, lower).wait_recv()
-    add_cross(lower)
+    lax.fori_loop(0, HEADS, add_lower, 0, unroll=4)
     all_of(4, back_c, prefix_c, lower).wait_send()
-    all_of(5, back_c, prefix_c, upper).wait_recv()
-    add_cross(upper)
-    all_of(5, back_c, prefix_c, upper).wait_send()
+
+    def add_upper(head, carry):
+        add_cross(head, upper)
+        return carry
+
+    all_of(LAST, back_c, prefix_c, upper).wait_recv()
+    lax.fori_loop(0, HEADS, add_upper, 0, unroll=8)
+    all_of(LAST, back_c, prefix_c, upper).wait_send()
 
 
 def on_device(queries, key_vectors, value_vectors, segment_ids, ridge_weight):
@@ -381,12 +401,14 @@
         kernel,
         name="mesa",
         out_shape=jax.ShapeDtypeStruct((ROWS, HEADS * WIDTH), F32),
-        in_specs=[hbm, hbm, hbm, vmem, pl.BlockSpec(memory_space=pltpu.SMEM)],
+        in_specs=[hbm] * 5,
         out_specs=vmem,
         scratch_shapes=[
             operand,
             operand,
             operand,
+            pltpu.VMEM((1, ROWS), jnp.int32),
+            pltpu.SMEM((HEADS,), F32),
             pltpu.VMEM((HEADS, WIDTH, ROWS), BF16),
             pltpu.VMEM((HEADS, INFO, WIDTH), F32),
             state_c,
@@ -405,7 +427,7 @@
             state_c,
             state_c,
             state_c,
-            pltpu.SemaphoreType.DMA((3,)),
+            pltpu.SemaphoreType.DMA((5,)),
             pltpu.SemaphoreType.DMA((6,)),
             pltpu.SemaphoreType.DMA((6,)),
             pltpu.SemaphoreType.DMA((3, 2)),
@@ -415,11 +437,16 @@
             collective_id=0, has_side_effects=True, vmem_limit_bytes=48 << 20
         ),
     )(
-        queries,
-        key_vectors,
-        value_vectors,
-        segment_ids.reshape(1, ROWS),
-        ridge_weight,
+        *(
+            pltpu.with_memory_space_constraint(value, pltpu.HBM)
+            for value in (
+                queries,
+                key_vectors,
+                value_vectors,
+                segment_ids.reshape(1, ROWS),
+                ridge_weight,
+            )
+        ),
     )
 
 

time: 53 us -> 45.4 us (0.86)
  local copies, waits for them, and re-layouts: 4.77 us -> 0.97 us
  Pallas kernels: 47.3 us -> 43.8 us
    unnamed x11 -> x1, local copies, waits for them, and re-layouts: 4.77 us -> 0.97 us
    pallas_call x1, Pallas kernels: 47.3 us -> 43.8 us  [on_device(): pl.pallas_call(kernel, name='mesa', out_shape=jax.ShapeDtypeStruct((ROWS,...]
where the time goes in v3:
time: 45.4 us; the launch traced here: 44.7 us
  Pallas kernels  43.8 us (96%)
  local copies, waits for them, and re-layouts  0.97 us (2%)
    pallas_call x1, Pallas kernels, on_device(): pl.pallas_call(kernel, name='mesa', out_shape=jax.ShapeDtypeStruct((ROWS,...  43.8 us
    unnamed x1, local copies, waits for them, and re-layouts  0.97 us

profile of v3, /device:TPU:0, one launch (start us, length us, event | category | flops | bytes accessed | tf_op | source)
XLA Modules:
  0.0 44.7 jit_solution(13903500196018446994)
XLA Ops:
  0.0 43.8 %mesa.1 = f32[128,2048]{1,0:T(8,128)S(1)} custom-call(bf16[128,2048]{1,0:T(8,128)(2,1)} %q_hbm.1, bf16[128,2048]{1,0:T(8,128)(2,1)} %k_hbm.1, bf16[128,2048]{1,0:T(8,128)(2,1)} %v_hbm.1, s32[1,128]{1,0:T(1,128)} %bitcast.1, f32[16]{0:T(128)} %ridge_hbm.1), custom_call_target="tpu_custom_call" | custom-call | tf_op jit(solution)/shard_map/mesa/pallas_call | solution.py:400
  43.8 1.0 %copy.7 = f32[128,2048]{1,0:T(8,128)} copy(f32[128,2048]{1,0:T(8,128)S(1)} %mesa.1) | data formatting | bytes 2097152

commit v4 on v3

--- a/solution.py
+++ b/solution.py
@@ -15,7 +15,8 @@
 INNER = 16
 OUTER = 8
 SIDE = 4
-GROUP = 4
+GROUP = 8
+STEPS = 4
 LAST = 5
 OFFSETS = sorted(
     ((x, z) for z in range(SIDE) for x in range(SIDE) if (x, z) != (0, 0)),
@@ -47,6 +48,32 @@
     return jnp.concatenate([value, value], 1)
 
 
+def cross_part(high, low, state):
+    state_high, state_low = halves(state)
+    return mm(
+        jnp.concatenate([high, low, high], 1),
+        jnp.concatenate([state_high, state_high, state_low], 0),
+    )
+
+
+def finish(part_ref, late_ref, state_ref, out_hbm, done, sems):
+    stores = []
+    for step in range(STEPS):
+        for head in range(step * HEADS // STEPS, (step + 1) * HEADS // STEPS):
+            late = late_ref[head]
+            cols = pl.ds(head * WIDTH, WIDTH)
+            done[:, cols] = part_ref[:, cols] + cross_part(
+                late[:, :HALF], late[:, HALF:], state_ref[head, HALF:]
+            )
+        cols = pl.ds(step * HEADS // STEPS * WIDTH, HEADS // STEPS * WIDTH)
+        stores.append(
+            pltpu.make_async_copy(done.at[:, cols], out_hbm.at[:, cols], sems.at[step])
+        )
+        stores[-1].start()
+    for store in stores:
+        store.wait()
+
+
 def kernel(
     q_hbm,
     k_hbm,
@@ -54,6 +81,8 @@
     seg_hbm,
     ridge_hbm,
     out_ref,
+    late_ref,
+    prefix_c,
     q_ref,
     k_ref,
     v_ref,
@@ -75,7 +104,6 @@
     back_g,
     prefix_g,
     back_c,
-    prefix_c,
     solved,
     load_sem,
     send_sem,
@@ -217,9 +245,13 @@
         first_local[head] = local + ridge_ref[head] * query
         return carry
 
+    def prepare_some(some):
+        for head in range(4 * some, 4 * some + 4):
+            prepare(head, 0)
+
     loads[3].wait()
     loads[4].wait()
-    lax.fori_loop(0, HEADS, prepare, 0, unroll=4)
+    prepare_some(0)
 
     def last_of(shard):
         return recv_g[shard, HALF + 1 : HALF + 2]
@@ -267,6 +299,7 @@
         info_row == 0, summed[HALF:PART], recv_g[INNER - 1, HALF:PART]
     )
     hand_on(0, total_g, early_g, sent)
+    prepare_some(1)
     take(0, total_g, early_g, sent)
     prefixes(recv_g, early_g, back_g, whole)
     start_all(3, back_g, prefix_g, returned, peers)
@@ -275,6 +308,7 @@
         all_of(kind, send_c, recv_c, rows).wait_recv()
         total_c[rows] = total_of(recv_c, rows)
         hand_on(kind, total_c, early_c, rows)
+        prepare_some(kind + 1)
         take(kind, total_c, early_c, rows)
         prefixes(recv_c, early_c, back_c, rows)
         start_all(kind + 3, back_c, prefix_c, rows, peers if kind == 1 else peers)
@@ -353,21 +387,16 @@
         out_ref[:, cols] = mm_split(scores, twice(v_ref[:, cols]))
         return carry
 
-    lax.fori_loop(0, HEADS, read_out, 0, unroll=4)
+    lax.fori_loop(0, HEADS, read_out, 0, unroll=8)
     carried = (seg_rows == first).astype(F32)
 
-    def add_cross(head, rows):
+    def add_lower(head, carry):
         cols = head_slice(head)
-        answer = solved[head, :, rows.start : rows.start + HALF] * carried[:, :HALF]
-        high, low = halves(answer)
-        cross_high, cross_low = halves(prefix_c[head, rows])
-        out_ref[:, cols] = out_ref[:, cols] + mm(
-            jnp.concatenate([high, low, high], 1),
-            jnp.concatenate([cross_high, cross_high, cross_low], 0),
+        high, low = halves(solved[head] * carried)
+        late_ref[head] = jnp.concatenate([high[:, HALF:], low[:, HALF:]], 1)
+        out_ref[:, cols] = out_ref[:, cols] + cross_part(
+            high[:, :HALF], low[:, :HALF], prefix_c[head, lower]
         )
-
-    def add_lower(head, carry):
-        add_cross(head, lower)
         return carry
 
     all_of(0, send_g, recv_g, sent).wait_send()
@@ -379,15 +408,10 @@
         pass_on(1, total_c, early_c, step, lower).wait_send()
         pass_on(2, total_c, early_c, step, upper).wait_send()
     all_of(4, back_c, prefix_c, lower).wait_recv()
-    lax.fori_loop(0, HEADS, add_lower, 0, unroll=4)
+    lax.fori_loop(0, HEADS, add_lower, 0, unroll=8)
     all_of(4, back_c, prefix_c, lower).wait_send()
 
-    def add_upper(head, carry):
-        add_cross(head, upper)
-        return carry
-
     all_of(LAST, back_c, prefix_c, upper).wait_recv()
-    lax.fori_loop(0, HEADS, add_upper, 0, unroll=8)
     all_of(LAST, back_c, prefix_c, upper).wait_send()
 
 
@@ -397,12 +421,16 @@
     operand = pltpu.VMEM((ROWS, HEADS * WIDTH), BF16)
     state_g = pltpu.VMEM((INNER, PART, WIDTH), F32)
     state_c = pltpu.VMEM((INNER, ROWS, WIDTH), F32)
-    return pl.pallas_call(
+    part, late, state = pl.pallas_call(
         kernel,
         name="mesa",
-        out_shape=jax.ShapeDtypeStruct((ROWS, HEADS * WIDTH), F32),
+        out_shape=(
+            jax.ShapeDtypeStruct((ROWS, HEADS * WIDTH), F32),
+            jax.ShapeDtypeStruct((HEADS, ROWS, WIDTH), BF16),
+            jax.ShapeDtypeStruct((INNER, ROWS, WIDTH), F32),
+        ),
         in_specs=[hbm] * 5,
-        out_specs=vmem,
+        out_specs=(vmem, vmem, vmem),
         scratch_shapes=[
             operand,
             operand,
@@ -424,7 +452,6 @@
             pltpu.VMEM((2, ROWS, WIDTH), F32),
             state_g,
             state_g,
-            state_c,
             state_c,
             state_c,
             pltpu.SemaphoreType.DMA((5,)),
@@ -448,6 +475,18 @@
             )
         ),
     )
+    return pl.pallas_call(
+        finish,
+        name="finish",
+        out_shape=jax.ShapeDtypeStruct((ROWS, HEADS * WIDTH), F32),
+        in_specs=[vmem, vmem, vmem],
+        out_specs=hbm,
+        scratch_shapes=[
+            pltpu.VMEM((ROWS, HEADS * WIDTH), F32),
+            pltpu.SemaphoreType.DMA((STEPS,)),
+        ],
+        compiler_params=pltpu.CompilerParams(vmem_limit_bytes=16 << 20),
+    )(part, late, state)
 
 
 def solution(mesh):

time: 45.4 us -> 44.4 us (0.978)
  local copies, waits for them, and re-layouts: 0.97 us -> 0 us
    unnamed x1 -> x0, local copies, waits for them, and re-layouts: 0.97 us -> none
    pallas_call x1 -> x2, Pallas kernels: 43.8 us -> 44.1 us  [the longest x1 42.9 us: on_device(): pl.pallas_call(kernel, name='mesa', out_shape=(jax.ShapeDtypeStruct((ROWS...]
where the time goes in v4:
time: 44.4 us; the launch traced here: 44.1 us
  Pallas kernels  44.1 us (99%)
    pallas_call x1, Pallas kernels, on_device(): pl.pallas_call(kernel, name='mesa', out_shape=(jax.ShapeDtypeStruct((ROWS...  42.9 us
    pallas_call x1, Pallas kernels, on_device(): pl.pallas_call(finish, name='finish', out_shape=jax.ShapeDtypeStruct((ROW...  1.22 us

profile of v4, /device:TPU:0, one launch (start us, length us, event | category | flops | bytes accessed | tf_op | source)
XLA Modules:
  0.0 44.1 jit_solution(1543479584639345481)
XLA Ops:
  0.0 42.9 %mesa.1 = (f32[128,2048]{1,0:T(8,128)S(1)}, bf16[16,128,128]{2,1,0:T(8,128)(2,1)S(1)}, f32[16,128,128]{2,1,0:T(8,128)S(1)}) custom-call(bf16[128,2048]{1,0:T(8,128)(2,1)} %q_hbm.1, bf16[128,2048]{1,0:T(8,128)(2,1)} %k_hbm.1, bf16[128,2048]{1,0:T(8,128)(2,1)} %v_hbm.1, s32[1,128]{1,0:T(1,128)} %bitcast.1, f32[16]{0:T(128)} %ridge_hbm.1), custom_call_target="tpu_custom_call" | custom-call | tf_op jit(solution)/shard_map/mesa/pallas_call | solution.py:424
  42.9 1.2 %finish.1 = f32[128,2048]{1,0:T(8,128)} custom-call(f32[128,2048]{1,0:T(8,128)S(1)} %get-tuple-element.8.part_ref, bf16[16,128,128]{2,1,0:T(8,128)(2,1)S(1)} %get-tuple-element.9.late_ref, f32[16,128,128]{2,1,0:T(8,128)S(1)} %get-tuple-element.10.state_ref), custom_call_target="tpu_custom_call" | custom-call | tf_op jit(solution)/shard_map/finish/pallas_call | solution.py:478

commit v5 on v4

--- a/solution.py
+++ b/solution.py
@@ -141,18 +141,32 @@
     for step in (-2, -1, 1, 2):
         pl.semaphore_signal(barrier, inc=1, device_id=(group_at(step), me), device_id_type=MESH)
 
-    ranked = [place + (place >= me).astype(jnp.int32) for place in range(INNER - 1)]
-
-    def start_all(kind, source, target, rows, order):
-        for peer in order:
-            pltpu.make_async_remote_copy(
-                src_ref=source.at[peer, rows],
-                dst_ref=target.at[me, rows],
-                send_sem=send_sem.at[kind],
-                recv_sem=recv_sem.at[kind],
-                device_id=(group, peer),
-                device_id_type=MESH,
-            ).start()
+    def send(kind, source, target, rows, peer):
+        return pltpu.make_async_remote_copy(
+            src_ref=source.at[peer, rows],
+            dst_ref=target.at[me, rows],
+            send_sem=send_sem.at[kind],
+            recv_sem=recv_sem.at[kind],
+            device_id=(group, peer),
+            device_id_type=MESH,
+        )
+
+    def start_last(kind, source, target, rows):
+        parity = lax.rem(me_z, 2)
+        for z in (parity, 1 - parity, 2 + parity, 3 - parity):
+            for step in (2, 1, 3):
+                peer = z * SIDE + lax.rem(me_x + step, SIDE)
+                send(kind, source, target, rows, peer).start()
+
+            @pl.when(z != me_z)
+            def _():
+                send(kind, source, target, rows, z * SIDE + me_x).start()
+
+        target[me, rows] = source[me, rows]
+
+    def start_all(kind, source, target, rows):
+        for peer in peers:
+            send(kind, source, target, rows, peer).start()
         target[me, rows] = source[me, rows]
 
     def all_of(kind, source, target, rows):
@@ -218,7 +232,7 @@
     loads[1].wait()
     lax.fori_loop(0, HEADS // 2, gram_pair, 0, unroll=2)
     pl.semaphore_wait(barrier, INNER - 1 + 4)
-    start_all(0, send_g, recv_g, sent, peers)
+    start_all(0, send_g, recv_g, sent)
 
     def cross(head, carry):
         turned = key_t[head].astype(F32) * (weight * scales[head, 0:1])
@@ -227,8 +241,8 @@
 
     loads[2].wait()
     lax.fori_loop(0, HEADS, cross, 0, unroll=4)
-    start_all(1, send_c, recv_c, lower, peers)
-    start_all(2, send_c, recv_c, upper, peers)
+    start_all(1, send_c, recv_c, lower)
+    start_all(2, send_c, recv_c, upper)
 
     def prepare(head, carry):
         cols = head_slice(head)
@@ -246,8 +260,7 @@
         return carry
 
     def prepare_some(some):
-        for head in range(4 * some, 4 * some + 4):
-            prepare(head, 0)
+        lax.fori_loop(4 * some, 4 * some + 4, prepare, 0, unroll=2)
 
     loads[3].wait()
     loads[4].wait()
@@ -302,7 +315,7 @@
     prepare_some(1)
     take(0, total_g, early_g, sent)
     prefixes(recv_g, early_g, back_g, whole)
-    start_all(3, back_g, prefix_g, returned, peers)
+    start_all(3, back_g, prefix_g, returned)
 
     for kind, rows in ((1, lower), (2, upper)):
         all_of(kind, send_c, recv_c, rows).wait_recv()
@@ -311,7 +324,7 @@
         prepare_some(kind + 1)
         take(kind, total_c, early_c, rows)
         prefixes(recv_c, early_c, back_c, rows)
-        start_all(kind + 3, back_c, prefix_c, rows, peers if kind == 1 else peers)
+        (start_last if kind + 3 == LAST else start_all)(kind + 3, back_c, prefix_c, rows)
 
     all_of(3, back_g, prefix_g, returned).wait_recv()
 

time: 44.4 us -> 43.8 us (0.986)
    pallas_call x1, Pallas kernels: 42.9 us -> 42.4 us  [on_device(): pl.pallas_call(kernel, name='mesa', out_shape=(jax.ShapeDtypeStruct((ROWS...]
where the time goes in v5:
time: 43.8 us; the launch traced here: 43.7 us
  Pallas kernels  43.7 us (100%)
    pallas_call x1, Pallas kernels, on_device(): pl.pallas_call(kernel, name='mesa', out_shape=(jax.ShapeDtypeStruct((ROWS...  42.4 us
    pallas_call x1, Pallas kernels, on_device(): pl.pallas_call(finish, name='finish', out_shape=jax.ShapeDtypeStruct((ROW...  1.22 us

profile of v5, /device:TPU:0, one launch (start us, length us, event | category | flops | bytes accessed | tf_op | source)
XLA Modules:
  0.0 43.7 jit_solution(7192313661180771355)
XLA Ops:
  0.0 42.4 %mesa.1 = (f32[128,2048]{1,0:T(8,128)S(1)}, bf16[16,128,128]{2,1,0:T(8,128)(2,1)S(1)}, f32[16,128,128]{2,1,0:T(8,128)S(1)}) custom-call(bf16[128,2048]{1,0:T(8,128)(2,1)} %q_hbm.1, bf16[128,2048]{1,0:T(8,128)(2,1)} %k_hbm.1, bf16[128,2048]{1,0:T(8,128)(2,1)} %v_hbm.1, s32[1,128]{1,0:T(1,128)} %bitcast.1, f32[16]{0:T(128)} %ridge_hbm.1), custom_call_target="tpu_custom_call" | custom-call | tf_op jit(solution)/shard_map/mesa/pallas_call | solution.py:437
  42.4 1.2 %finish.1 = f32[128,2048]{1,0:T(8,128)} custom-call(f32[128,2048]{1,0:T(8,128)S(1)} %get-tuple-element.8.part_ref, bf16[16,128,128]{2,1,0:T(8,128)(2,1)S(1)} %get-tuple-element.9.late_ref, f32[16,128,128]{2,1,0:T(8,128)S(1)} %get-tuple-element.10.state_ref), custom_call_target="tpu_custom_call" | custom-call | tf_op jit(solution)/shard_map/finish/pallas_call | solution.py:491

commit v6 on v5

--- a/solution.py
+++ b/solution.py
@@ -132,14 +132,13 @@
             )
         )
     ]
-    for load in loads:
-        load.start()
-
     barrier = pltpu.get_barrier_semaphore()
     for peer in peers:
         pl.semaphore_signal(barrier, inc=1, device_id=(group, peer), device_id_type=MESH)
     for step in (-2, -1, 1, 2):
         pl.semaphore_signal(barrier, inc=1, device_id=(group_at(step), me), device_id_type=MESH)
+    for load in loads:
+        load.start()
 
     def send(kind, source, target, rows, peer):
         return pltpu.make_async_remote_copy(

time: 43.8 us -> 43.8 us (level)
  no operation moved by 1% of the time
where the time goes in v6:
time: 43.8 us; the launch traced here: 43.7 us
  Pallas kernels  43.7 us (100%)
    pallas_call x1, Pallas kernels, on_device(): pl.pallas_call(kernel, name='mesa', out_shape=(jax.ShapeDtypeStruct((ROWS...  42.4 us
    pallas_call x1, Pallas kernels, on_device(): pl.pallas_call(finish, name='finish', out_shape=jax.ShapeDtypeStruct((ROW...  1.23 us

profile of v6, /device:TPU:0, one launch (start us, length us, event | category | flops | bytes accessed | tf_op | source)
XLA Modules:
  0.0 43.7 jit_solution(10511417133015787710)
XLA Ops:
  0.0 42.4 %mesa.1 = (f32[128,2048]{1,0:T(8,128)S(1)}, bf16[16,128,128]{2,1,0:T(8,128)(2,1)S(1)}, f32[16,128,128]{2,1,0:T(8,128)S(1)}) custom-call(bf16[128,2048]{1,0:T(8,128)(2,1)} %q_hbm.1, bf16[128,2048]{1,0:T(8,128)(2,1)} %k_hbm.1, bf16[128,2048]{1,0:T(8,128)(2,1)} %v_hbm.1, s32[1,128]{1,0:T(1,128)} %bitcast.1, f32[16]{0:T(128)} %ridge_hbm.1), custom_call_target="tpu_custom_call" | custom-call | tf_op jit(solution)/shard_map/mesa/pallas_call | solution.py:436
  42.4 1.2 %finish.1 = f32[128,2048]{1,0:T(8,128)} custom-call(f32[128,2048]{1,0:T(8,128)S(1)} %get-tuple-element.8.part_ref, bf16[16,128,128]{2,1,0:T(8,128)(2,1)S(1)} %get-tuple-element.9.late_ref, f32[16,128,128]{2,1,0:T(8,128)S(1)} %get-tuple-element.10.state_ref), custom_call_target="tpu_custom_call" | custom-call | tf_op jit(solution)/shard_map/finish/pallas_call | solution.py:490

commit v7 on v6

--- a/solution.py
+++ b/solution.py
@@ -152,8 +152,8 @@
 
     def start_last(kind, source, target, rows):
         parity = lax.rem(me_z, 2)
-        for z in (parity, 1 - parity, 2 + parity, 3 - parity):
-            for step in (2, 1, 3):
+        for turn, z in enumerate((parity, 1 - parity, 3 - parity, 2 + parity)):
+            for step in (2, 1, 3) if turn % 2 == 0 else (2, 3, 1):
                 peer = z * SIDE + lax.rem(me_x + step, SIDE)
                 send(kind, source, target, rows, peer).start()
 

time: 43.8 us -> 43.8 us (level)
  no operation moved by 1% of the time
where the time goes in v7:
time: 43.8 us; the launch traced here: 43.7 us
  Pallas kernels  43.7 us (100%)
    pallas_call x1, Pallas kernels, on_device(): pl.pallas_call(kernel, name='mesa', out_shape=(jax.ShapeDtypeStruct((ROWS...  42.4 us
    pallas_call x1, Pallas kernels, on_device(): pl.pallas_call(finish, name='finish', out_shape=jax.ShapeDtypeStruct((ROW...  1.23 us

profile of v7, /device:TPU:0, one launch (start us, length us, event | category | flops | bytes accessed | tf_op | source)
XLA Modules:
  0.0 43.7 jit_solution(7335715926453202727)
XLA Ops:
  0.0 42.4 %mesa.1 = (f32[128,2048]{1,0:T(8,128)S(1)}, bf16[16,128,128]{2,1,0:T(8,128)(2,1)S(1)}, f32[16,128,128]{2,1,0:T(8,128)S(1)}) custom-call(bf16[128,2048]{1,0:T(8,128)(2,1)} %q_hbm.1, bf16[128,2048]{1,0:T(8,128)(2,1)} %k_hbm.1, bf16[128,2048]{1,0:T(8,128)(2,1)} %v_hbm.1, s32[1,128]{1,0:T(1,128)} %bitcast.1, f32[16]{0:T(128)} %ridge_hbm.1), custom_call_target="tpu_custom_call" | custom-call | tf_op jit(solution)/shard_map/mesa/pallas_call | solution.py:436
  42.4 1.2 %finish.1 = f32[128,2048]{1,0:T(8,128)} custom-call(f32[128,2048]{1,0:T(8,128)S(1)} %get-tuple-element.8.part_ref, bf16[16,128,128]{2,1,0:T(8,128)(2,1)S(1)} %get-tuple-element.9.late_ref, f32[16,128,128]{2,1,0:T(8,128)S(1)} %get-tuple-element.10.state_ref), custom_call_target="tpu_custom_call" | custom-call | tf_op jit(solution)/shard_map/finish/pallas_call | solution.py:490
